TPU v7x, 128 devices: a whole 4x4x4 slice. The times are simulated.
128 devices in a mesh: dp: 16 (over z, x), tensor: 8 (over y, core).
Axes of the slice: x: 4, y: 4, z: 4, core: 2. Of those that a mesh axis runs over, the one named last changes fastest.
Arguments:
- tokens: bfloat16 [128, 128, 8192], P('dp', None, 'tensor'), may hold values from -6 to 6
- shared_prefix_tokens: bfloat16 [16, 256, 8192], P('dp', None, 'tensor'), may hold values from -6 to 6
- input_norm_gain: bfloat16 [8192], replicated, may hold values from 0.5 to 8
- query_weight: bfloat16 [8192, 8192], P(None, 'tensor'), may hold values from -0.0625 to 0.0625
- key_weight: bfloat16 [8192, 1024], P(None, 'tensor'), may hold values from -0.0625 to 0.0625
- value_weight: bfloat16 [8192, 1024], P(None, 'tensor'), may hold values from -0.0625 to 0.0625
- adapter_down_weight: bfloat16 [64, 8192, 16], P('dp', 'tensor'), may hold values from -0.0625 to 0.0625
- adapter_up_weight: bfloat16 [64, 16, 8192], P('dp', None, 'tensor'), may hold values from -0.75 to 0.75
- adapter_position: int32 [64], replicated, may hold values from 0 to 63, as said below
- request_adapter: int32 [128], P('dp'), may hold values from 0 to 63, as said below
- request_group: int32 [128], P('dp'), may hold values from 0 to 15
- lengths: int32 [128], P('dp'), may hold values from 1 to 128
- request_page_table: int32 [128, 1], P('dp'), may hold values from 0 to 127, as said below
Outputs:
- context: bfloat16 [128, 128, 8192], P('dp', None, 'tensor')
- paged_key_values: bfloat16 [128, 2, 128, 1024], P('dp', None, None, 'tensor')
Inputs may be any that keep to these rules, and one draw needn't show every extreme that they name: A permutation: adapter a is held at slot adapter_position[a], on index adapter_position[a] // 4 of dp. `request_adapter`: the 8 requests of one index of dp use adapters held by 8 different indices of dp. `request_page_table`: the requests of index i of dp use the pages i * 8 to (i + 1) * 8 - 1, each page once.
All inputs are finite; a program needn't handle non-finite values.
Results may differ from a plain program's by a relative error of at most 0.011.
The roundings to bfloat16 on the way count: a program that leaves them out, or rounds other values in their place, can miss the bound.
Values may be sent and summed in bfloat16 or wider, within the bound.
No kernel may reach another device: no remote copies, remote signals or barrier semaphores. Data moves between devices by JAX's collectives and lax.ppermute only.
A program may use at most 128 MiB of HBM per device.

v0:
```python
import jax
import jax.numpy as jnp
from jax import lax
from jax.sharding import PartitionSpec as P

HEAD_WIDTH = 128
ADAPTER_RANK = 16
PAGE_TOKENS = 128
EPS = 1e-05
THETA = 500000.0
ADAPTER_SCALE = 2.0


def rope_tables(positions, width):
    half = width // 2
    freq = THETA ** (-(jnp.arange(half, dtype=jnp.float32) * 2.0 / width))
    angle = positions.astype(jnp.float32)[:, None] * freq[None, :]
    return (jnp.cos(angle), jnp.sin(angle))


def apply_rope(values, cosine, sine):
    half = values.shape[-1] // 2
    first = values[..., :half]
    second = values[..., half:]
    cos_b = cosine[:, None, :]
    sin_b = sine[:, None, :]
    return jnp.concatenate(
        [first * cos_b - second * sin_b, second * cos_b + first * sin_b], axis=-1
    )


def normalize(rows, gain):
    values = rows.astype(jnp.float32)
    scale = lax.rsqrt(jnp.mean(values * values, axis=-1, keepdims=True) + EPS)
    return (values * scale * gain.astype(jnp.float32)).astype(jnp.bfloat16)


def on_device(
    tokens,
    shared_prefix_tokens,
    input_norm_gain,
    query_weight,
    key_weight,
    value_weight,
    adapter_down_weight,
    adapter_up_weight,
    adapter_position,
    request_adapter,
    request_group,
    lengths,
    request_page_table,
):
    req_dev, seq_len, d_part = tokens.shape
    grp_dev, pre_len, _ = shared_prefix_tokens.shape
    q_width = query_weight.shape[1]
    kv_width = key_weight.shape[1]
    q_heads = q_width // HEAD_WIDTH
    kv_local = kv_width // HEAD_WIDTH
    group_members = q_heads // kv_local
    token_rows = req_dev * seq_len
    column = lax.axis_index("tensor")
    place = lax.axis_index("dp")
    full_tokens, full_prefix = (
        lax.all_gather(tokens.reshape(token_rows, d_part), "tensor", axis=1, tiled=True),
        lax.all_gather(
            shared_prefix_tokens.reshape(grp_dev * pre_len, d_part), "tensor", axis=1, tiled=True
        ),
    )
    normed_input = normalize(full_tokens, input_norm_gain)
    prefix_normed = normalize(full_prefix, input_norm_gain)
    pre_cos, pre_sin = rope_tables(jnp.arange(pre_len), HEAD_WIDTH)
    pre_keys = jnp.dot(prefix_normed, key_weight, preferred_element_type=jnp.float32).reshape(
        grp_dev, pre_len, kv_local, HEAD_WIDTH
    )
    pre_keys = (
        apply_rope(pre_keys, pre_cos, pre_sin)
        .astype(jnp.bfloat16)
        .reshape(grp_dev, pre_len, kv_width)
    )
    pre_vals = (
        jnp.dot(prefix_normed, value_weight, preferred_element_type=jnp.float32)
        .astype(jnp.bfloat16)
        .reshape(grp_dev, pre_len, kv_width)
    )
    all_pairs = lax.all_gather(jnp.stack([pre_keys, pre_vals], 1), "dp", axis=0, tiled=True)
    table_ids = jnp.arange(adapter_position.shape[0])
    slots = jnp.sum(
        jnp.where(request_adapter[:, None] == table_ids[None, :], adapter_position[None, :], 0),
        axis=1,
    )
    local_rows = lax.dynamic_slice_in_dim(normed_input, column * d_part, d_part, 1)
    row_slot = jnp.repeat(slots, seq_len)
    page_piece = lax.all_gather(adapter_down_weight, "dp", axis=0, tiled=True)
    count = page_piece.shape[0]
    part = jnp.einsum("td,ndr->tnr", local_rows, page_piece, preferred_element_type=jnp.float32)
    pick = row_slot[:, None] == jnp.arange(count)[None, :]
    partial_low = jnp.sum(jnp.where(pick[:, :, None], part, 0.0), axis=1)
    low_rank_rows = lax.psum(partial_low, "tensor").astype(jnp.bfloat16)
    page_piece = lax.all_gather(adapter_up_weight, "dp", axis=0, tiled=True)
    count = page_piece.shape[0]
    pick = (row_slot[:, None] == jnp.arange(count)[None, :]).astype(jnp.bfloat16)
    spread = (pick[:, :, None] * low_rank_rows[:, None, :]).reshape(
        token_rows, count * ADAPTER_RANK
    )
    summed_rows = jnp.dot(
        spread,
        page_piece.reshape(count * ADAPTER_RANK, q_width),
        preferred_element_type=jnp.float32,
    )
    adapter_term = (ADAPTER_SCALE * summed_rows).astype(jnp.bfloat16)
    own_cos, own_sin = rope_tables(pre_len + jnp.arange(seq_len), HEAD_WIDTH)
    query_rows = jnp.dot(
        normed_input, query_weight, preferred_element_type=jnp.float32
    ) + adapter_term.astype(jnp.float32)
    query_rows = apply_rope(
        query_rows.reshape(req_dev, seq_len, q_heads, HEAD_WIDTH), own_cos, own_sin
    ).astype(jnp.bfloat16)
    key_rows = jnp.dot(normed_input, key_weight, preferred_element_type=jnp.float32).reshape(
        req_dev, seq_len, kv_local, HEAD_WIDTH
    )
    key_rows = apply_rope(key_rows, own_cos, own_sin).astype(jnp.bfloat16)
    value_rows = (
        jnp.dot(normed_input, value_weight, preferred_element_type=jnp.float32)
        .astype(jnp.bfloat16)
        .reshape(req_dev, seq_len, kv_local, HEAD_WIDTH)
    )
    live = jnp.arange(seq_len)[None, :] < lengths[:, None]
    key_rows = jnp.where(live[:, :, None, None], key_rows, jnp.zeros_like(key_rows))
    value_rows = jnp.where(live[:, :, None, None], value_rows, jnp.zeros_like(value_rows))
    chosen = all_pairs[request_group]
    all_keys = jnp.concatenate(
        [chosen[:, 0].reshape(req_dev, pre_len, kv_local, HEAD_WIDTH), key_rows], 1
    )
    all_vals = jnp.concatenate(
        [chosen[:, 1].reshape(req_dev, pre_len, kv_local, HEAD_WIDTH), value_rows], 1
    )
    grouped_query = query_rows.reshape(req_dev, seq_len, kv_local, group_members, HEAD_WIDTH)
    scores = jnp.einsum(
        "btkgd,bskd->bkgts", grouped_query, all_keys, preferred_element_type=jnp.float32
    ) * HEAD_WIDTH ** (-0.5)
    seen = jnp.arange(pre_len + seq_len)[None, :]
    allowed = (seen < pre_len) | (seen - pre_len <= jnp.arange(seq_len)[:, None])
    scores = jnp.where(allowed[None, None, None], scores, -1e30)
    top = jnp.max(scores, axis=-1, keepdims=True)
    weights = jnp.exp(scores - top)
    probs = (weights / jnp.sum(weights, axis=-1, keepdims=True)).astype(jnp.bfloat16)
    attention_output = jnp.einsum(
        "bkgts,bskd->btkgd", probs, all_vals, preferred_element_type=jnp.float32
    )
    attention_output = jnp.where(live[:, :, None, None, None], attention_output, 0.0)
    context = attention_output.reshape(req_dev, seq_len, q_width).astype(jnp.bfloat16)
    pages_req = seq_len // PAGE_TOKENS
    page_blocks = jnp.stack(
        [
            key_rows.reshape(req_dev, pages_req, PAGE_TOKENS, kv_width),
            value_rows.reshape(req_dev, pages_req, PAGE_TOKENS, kv_width),
        ],
        2,
    )
    page_blocks = page_blocks.reshape(req_dev * pages_req, 2, PAGE_TOKENS, kv_width)
    local_page = request_page_table.reshape(-1) - place * (req_dev * pages_req)
    paged_key_values = jnp.zeros_like(page_blocks).at[local_page].set(page_blocks)
    return (context, paged_key_values)


def solution(mesh):
    in_specs = (
        P("dp", None, "tensor"),
        P("dp", None, "tensor"),
        P(),
        P(None, "tensor"),
        P(None, "tensor"),
        P(None, "tensor"),
        P("dp", "tensor", None),
        P("dp", None, "tensor"),
        P(),
        P("dp"),
        P("dp"),
        P("dp"),
        P("dp", None),
    )
    out_specs = (P("dp", None, "tensor"), P("dp", None, None, "tensor"))
    return jax.shard_map(
        on_device, mesh=mesh, in_specs=in_specs, out_specs=out_specs, check_vma=False
    )
```

profile of v0, /device:TPU:0, one launch (start us, length us, event | category | flops | bytes accessed | tf_op | source)
XLA Modules:
  0.0 344.5 jit_solution(120121396503228455)
XLA Ops:
  7.2 0.7 all-gather.15.cloned.1.call-update
  8.0 0.7 convert_element_type.114
  8.7 35.6 %all-gather.15.cloned.1.call-done = bf16[1,256,8192]{2,1,0:T(8,128)(2,1)} async-done(((bf16[1,256,1024]{2,1,0:T(8,128)(2,1)}), bf16[1,256,8192]{2,1,0:T(8,128)(2,1)}) %all-gather.15.cloned.1.call-update) | async-done | bytes 4194320 | tf_op jit(solution)/shard_map/all_gather | solution.py:65
  44.3 3.3 fusion.5
  47.6 0.2 copy-done.4
  47.8 3.3 fusion.33
  51.1 0.3 fusion.58
  51.5 1.7 fusion.39
  53.3 0.8 copy.63
  54.1 0.7 all-gather.9.cloned.1.call-update
  54.9 0.5 all-gather.11.cloned.1.call-update
  55.4 0.5 all-gather.13.cloned.1.call-update
  56.0 0.2 select_reduce_fusion.1
  56.4 0.3 multiply_cosine_fusion
  56.7 0.6 iota_compare_fusion.3
  57.3 0.6 pad_clamp_fusion
  57.9 0.2 fusion.48
  58.1 0.5 fusion.59
  58.6 40.8 %all-gather.7.cloned.1.call-done = bf16[16,2,256,128]{3,2,1,0:T(8,128)(2,1)} async-done(((bf16[1,2,256,128]{3,2,1,0:T(8,128)(2,1)}), bf16[16,2,256,128]{3,2,1,0:T(8,128)(2,1)}) %all-gather.7.cloned.1.call-update) | async-done | bytes 2097168 | tf_op jit(solution)/shard_map/all_gather | solution.py:85
  99.4 2.5 gather_fusion
  101.9 1.0 fusion.67
  102.9 2.0 copy.78
  105.0 80.4 %all-gather.9.cloned.1.call-done = bf16[1024,8192]{1,0:T(8,128)(2,1)} async-done(((bf16[1024,1024]{1,0:T(8,128)(2,1)}), bf16[1024,8192]{1,0:T(8,128)(2,1)}) %all-gather.9.cloned.1.call-update) | async-done | bytes 16777232 | tf_op jit(solution)/shard_map/all_gather | solution.py:64
  185.4 7.5 %fusion = f32[1024]{0:T(1024)S(1)} fusion(bf16[1024,8192]{1,0:T(8,128)(2,1)} %all-gather.9.cloned.1.call-done), kind=kLoop, calls=%fused_computation.4 | loop fusion | flops 25164800 | bytes 16781312 | tf_op jit(solution)/shard_map/reduce_sum | solution.py:34
  192.9 3.2 copy-done.2
  196.0 8.3 %fusion.2 = bf16[1024,8192]{1,0:T(8,128)(2,1)} fusion(bf16[1024,8192]{1,0:T(8,128)(2,1)S(1)} %copy-done.2, f32[8192]{0:T(1024)S(1)} %convert_element_type.114, f32[1024]{0:T(1024)S(1)} %add_rsqrt_fusion), kind=kLoop, calls=%fused_computation.6 | loop fusion | flops 33554432 | bytes 33591296 | tf_op jit(solution)/shard_map/convert_element_type | solution.py:35
  204.3 29.0 %all-gather.11.cloned.1.call-done = bf16[64,1024,16]{1,2,0:T(8,128)(2,1)} async-done(((bf16[4,1024,16]{1,2,0:T(8,128)(2,1)}), bf16[64,1024,16]{1,2,0:T(8,128)(2,1)}) %all-gather.11.cloned.1.call-update) | async-done | bytes 2097168 | tf_op jit(solution)/shard_map/all_gather | solution.py:93
  233.3 5.1 %select_reduce_fusion = f32[1024,16]{0,1:T(8,128)S(1)} fusion(pred[1024,64]{0,1:T(8,128)(4,1)S(1)} %get-tuple-element.23, bf16[64,1024,16]{1,2,0:T(8,128)(2,1)} %all-gather.11.cloned.1.call-done, bf16[1024,8192]{1,0:T(8,128)(2,1)} %fusion.2, s32[]{:T(128)S(6)} %select_n.72), kind=kOutput, calls=%fused_computation.27 | convolution fusion | flops 2149564416 | bytes 4325380 | tf_op jit(solution)/shard_map/td,ndr->tnr/dot_general | solution.py:95
  238.4 25.3 %psum.7 = bf16[1024,16]{0,1:T(8,128)(2,1)S(1)} all-reduce(f32[1024,16]{0,1:T(8,128)S(1)} %select_reduce_fusion), channel_id=1, replica_groups=mesh['dp'=16,'tensor'=8] {'tensor'}, use_global_device_ids=true, to_apply=%region_4.5 | all-reduce | flops 16384 | bytes 98304 | tf_op jit(solution)/shard_map/psum | solution.py:98
  263.7 8.5 %convolution_convert_fusion = bf16[1024,128]{1,0:T(8,128)(2,1)S(1)} fusion(bf16[1024,8192]{1,0:T(8,128)(2,1)} %fusion.2, bf16[8192,128]{1,0:T(8,128)(2,1)S(1)} %copy-done), kind=kOutput, calls=%fused_computation.38 | convolution fusion | flops 2147614720 | bytes 19136512 | tf_op jit(solution)/shard_map/dot_general | solution.py:123
  272.2 2.4 copy-done.3
  274.6 0.6 copy-done.11
  275.2 4.5 %fusion.68 = f32[1024,128]{1,0:T(8,128)S(1)} fusion(bf16[1024,8192]{1,0:T(8,128)(2,1)S(1)} %copy-done.3, bf16[8192,128]{1,0:T(8,128)(2,1)S(1)} %copy-done.11), kind=kOutput, calls=%fused_computation.101 | convolution fusion | flops 2147483648 | bytes 19398656 | tf_op jit(solution)/shard_map/dot_general | solution.py:118
  279.8 5.4 %fusion.12 = bf16[1024,1024]{1,0:T(8,128)(2,1)S(1)} fusion(bf16[64,16,1024]{2,1,0:T(8,128)(2,1)} %all-gather.13.cloned.1.call-done, bf16[1024,16]{0,1:T(8,128)(2,1)S(1)} %psum.7, bf16[1024,64]{0,1:T(8,128)(2,1)S(1)} %get-tuple-element.22), kind=kOutput, calls=%fused_computation.23 | convolution fusion | flops 2150629376 | bytes 4358144 | tf_op jit(solution)/shard_map/dot_general | solution.py:105
  285.3 22.6 %add_bitcast_fusion = f32[128,8,8,128]{3,1,2,0:T(8,128)S(1)} fusion(bf16[1024,1024]{1,0:T(8,128)(2,1)S(1)} %fusion.12, bf16[1024,8192]{1,0:T(8,128)(2,1)} %fusion.2, bf16[8192,1024]{1,0:T(8,128)(2,1)} %param.16), kind=kOutput, calls=%fused_computation.26 | convolution fusion | flops 17181966336 | bytes 39845888 | tf_op jit(solution)/shard_map/dot_general | solution.py:112
  307.9 1.0 copy.82
  308.9 4.6 %fusion.66 = (f32[8,128,8,64]{3,2,1,0:T(8,128)}, f32[8,128,8,64]{3,2,1,0:T(8,128)}) fusion(f32[8,128,8,128]{3,2,1,0:T(8,128)S(1)} %bitcast.99), kind=kLoop, calls=%fused_computation.99 | loop fusion | bytes 8388608 | tf_op jit(solution)/shard_map/slice | solution.py:23
  313.4 0.2 subtract_convert_fusion.1
  313.7 0.3 broadcast_select_fusion.1
  314.0 0.8 copy.65
  314.9 5.2 %subtract_convert_fusion = (bf16[8,128,8,64]{3,1,2,0:T(8,128)(2,1)S(1)}, bf16[8,128,8,64]{3,1,2,0:T(8,128)(2,1)S(1)}) fusion(f32[8,128,8,64]{3,2,1,0:T(8,128)} %get-tuple-element.15, f32[8,128,8,64]{3,2,1,0:T(8,128)} %get-tuple-element.14, f32[128,64]{1,0:T(8,128)S(1)} %get-tuple-element.29, f32[128,64]{1,0:T(8,128)S(1)} %get-tuple-element.28), kind=kLoop, calls=%fused_computation.25 | loop fusion | flops 4194304 | bytes 6356992 | tf_op jit(solution)/shard_map/convert.4
  320.1 3.1 fusion.4
  323.2 3.2 fusion.3
  326.5 5.3 %fusion.11 = bf16[8,1,128,8,128]{4,2,3,0,1:T(8,128)(2,1)} fusion(f32[8,8,128]{2,1,0:T(8,128)S(1)} %fusion.3, f32[8,8,128]{2,1,0:T(8,128)S(1)} %get-tuple-element.30, f32[8,384,128,8]{2,1,3,0:T(8,128)S(1)} %get-tuple-element.31, pred[128,384]{0,1:T(8,128)(4,1)S(1)} %fusion.48, pred[8,128]{1,0:T(8,128)(4,1)S(1)} %copy-done.9, ...), kind=kOutput, calls=%fused_computation.21 | convolution fusion | flops 824705024 | bytes 15582208 | tf_op jit(solution)/shard_map/bkgts,bskd->btkgd/dot_general | solution.py:147
  331.7 4.1 %copy.73 = bf16[8,128,1024]{2,1,0:T(8,128)(2,1)} copy(bf16[8,128,1024]{1,2,0:T(8,128)(2,1)} %bitcast.103) | data formatting | bytes 4194304
  335.8 0.3 maximum_select_fusion.1
  336.3 0.9 scatter_fusion
  337.2 0.8 copy-done.6
  (50 shorter events, 0.8 us)
Async XLA Ops:
  7.2 44.3 %copy-start = (bf16[8192,128]{1,0:T(8,128)(2,1)S(1)}, bf16[8192,128]{1,0:T(8,128)(2,1)}, u32[]{:S(2)}) copy-start(bf16[8192,128]{1,0:T(8,128)(2,1)} %param.18) | copy-start | bytes 6291460
  7.2 37.2 %all-gather.15.cloned.1.call-start = ((), (), s32[]{:S(2)}) async-start(), calls=%async_computation.4 | async-start | bytes 4718592 | tf_op jit(solution)/shard_map/all_gather | solution.py:65
  7.9 91.5 %all-gather.7.cloned.1.call-start = ((), (), s32[]{:S(2)}) async-start(), calls=%async_computation | async-start | bytes 2228224 | tf_op jit(solution)/shard_map/all_gather | solution.py:85
  44.3 3.4 %copy-start.4 = (bf16[1,256,8192]{2,1,0:T(8,128)(2,1)S(1)}, bf16[1,256,8192]{2,1,0:T(8,128)(2,1)}, u32[]{:S(2)}) copy-start(bf16[1,256,8192]{2,1,0:T(8,128)(2,1)} %all-gather.15.cloned.1.call-done) | copy-start | bytes 12582916
  51.5 4.6 %copy-start.12 = (s32[64]{0:T(128)S(1)}, s32[64]{0:T(128)}, u32[]{:S(2)}) copy-start(s32[64]{0:T(128)} %param.21) | copy-start | bytes 772
  51.5 4.6 %copy-start.13 = (s32[8]{0:T(128)S(1)}, s32[8]{0:T(128)}, u32[]{:S(2)}) copy-start(s32[8]{0:T(128)} %param.22) | copy-start | bytes 100
  51.5 5.2 %copy-start.14 = (s32[8]{0:T(128)S(1)}, s32[8]{0:T(128)}, u32[]{:S(2)}) copy-start(s32[8]{0:T(128)} %param.24) | copy-start | bytes 100
  51.5 5.8 %copy-start.15 = (s32[8]{0:T(128)S(1)}, s32[8]{0:T(128)}, u32[]{:S(2)}) copy-start(s32[8]{0:T(128)} %param.23) | copy-start | bytes 100
  51.5 6.6 %copy-start.16 = (s32[8,1]{0,1:T(1,128)S(1)}, s32[8,1]{0,1:T(1,128)}, u32[]{:S(2)}) copy-start(s32[8,1]{0,1:T(1,128)} %param.25) | copy-start | bytes 100
  54.1 131.3 %all-gather.9.cloned.1.call-start = ((), (), s32[]{:S(2)}) async-start(), calls=%async_computation.1 | async-start | bytes 18874368 | tf_op jit(solution)/shard_map/all_gather | solution.py:64
  54.8 178.5 %all-gather.11.cloned.1.call-start = ((), (), s32[]{:S(2)}) async-start(), calls=%async_computation.2 | async-start | bytes 2228224 | tf_op jit(solution)/shard_map/all_gather | solution.py:93
  55.4 224.4 %all-gather.13.cloned.1.call-start = ((), (), s32[]{:S(2)}) async-start(), calls=%async_computation.3 | async-start | bytes 2228224 | tf_op jit(solution)/shard_map/all_gather | solution.py:99
  185.4 10.7 %copy-start.2 = (bf16[1024,8192]{1,0:T(8,128)(2,1)S(1)}, bf16[1024,8192]{1,0:T(8,128)(2,1)}, u32[]{:S(2)}) copy-start(bf16[1024,8192]{1,0:T(8,128)(2,1)} %all-gather.9.cloned.1.call-done) | copy-start | bytes 50331652
  263.7 10.9 %copy-start.3 = (bf16[1024,8192]{1,0:T(8,128)(2,1)S(1)}, bf16[1024,8192]{1,0:T(8,128)(2,1)}, u32[]{:S(2)}) copy-start(bf16[1024,8192]{1,0:T(8,128)(2,1)} %fusion.2) | copy-start | bytes 50331652
  263.7 11.5 %copy-start.11 = (bf16[8192,128]{1,0:T(8,128)(2,1)S(1)}, bf16[8192,128]{1,0:T(8,128)(2,1)}, u32[]{:S(2)}) copy-start(bf16[8192,128]{1,0:T(8,128)(2,1)} %param.17) | copy-start | bytes 6291460
  308.9 4.8 %copy-start.9 = (pred[8,128]{1,0:T(8,128)(4,1)S(1)}, pred[8,128]{1,0:T(8,128)(4,1)}, u32[]{:S(2)}) copy-start(pred[8,128]{1,0:T(8,128)(4,1)} %iota_compare_fusion.3) | copy-start | bytes 3076
  314.9 5.2 %copy-start.5 = (bf16[8,256,1,128]{3,1,0,2:T(8,128)(2,1)S(1)}, bf16[8,256,1,128]{3,1,0,2:T(8,128)(2,1)}, u32[]{:S(2)}) copy-start(bf16[8,256,1,128]{3,1,0,2:T(8,128)(2,1)} %get-tuple-element.17) | copy-start | bytes 1572868
  323.2 3.2 copy-start.7
  323.2 3.2 copy-start.8
  331.7 4.6 %copy-start.10 = (s32[8]{0:T(128)S(1)}, s32[8]{0:T(128)}, u32[]{:S(2)}) copy-start(s32[8]{0:T(128)} %fusion.59) | copy-start | bytes 100
  331.7 6.2 %copy-start.1 = (bf16[8192,128]{1,0:T(8,128)(2,1)S(1)}, bf16[8192,128]{1,0:T(8,128)(2,1)}, u32[]{:S(2)}) copy-start(bf16[8192,128]{1,0:T(8,128)(2,1)} %param.18) | copy-start | bytes 6291460
  337.2 0.8 copy-start.6
Sparse Core Ops, SparseCore 0:
  9.7 34.5 all-gather.14
  54.2 45.1 all-gather.6
  101.1 84.1 all-gather.8
  187.4 45.8 all-gather.10
  235.3 44.5 all-gather.12
where the time goes:
time: 345 us
  waiting for transfers between devices  188 us (54%)
  matrix products  59.5 us (17%)
  other arithmetic  31.9 us (9%)
  blocking collectives  25.3 us (7%)
  local copies, waits for them, and re-layouts  25.1 us (7%)
  between operations  14.2 us (4%)
    all_gather x1, waiting for transfers between devices, on_device(): lax.all_gather(tokens.reshape(token_rows, d_part), 'tensor', axis=1, tile...  80.4 us
    all_gather x1, waiting for transfers between devices, on_device(): lax.all_gather(jnp.stack([pre_keys, pre_vals], 1), 'dp', axis=0, tiled=True)  40.8 us
    all_gather x1, waiting for transfers between devices, on_device(): lax.all_gather(shared_prefix_tokens.reshape(grp_dev * pre_len, d_part), '...  35.6 us
    all_gather x1, waiting for transfers between devices, on_device(): page_piece = lax.all_gather(adapter_down_weight, 'dp', axis=0, tiled=True)  29 us
    psum x1, blocking collectives, on_device(): low_rank_rows = lax.psum(partial_low, 'tensor').astype(jnp.bfloat16)  25.3 us
    dot_general x1, matrix products, on_device(): jnp.dot(normed_input, query_weight, preferred_element_type=jnp.float32)  22.6 us
    unnamed x37, local copies, waits for them, and re-layouts  14.3 us
    reduce_sum x2, other arithmetic, normalize(): scale = lax.rsqrt(jnp.mean(values * values, axis=-1, keepdims=True) + EPS)  10.7 us
  transfers between devices with their start and end apart: 5, of which 5 were waited for; matrix products, arithmetic and copies ran while one was open for 12% of the time, Pallas kernels for 0%

commit v1 on v0

--- a/solution.py
+++ b/solution.py
@@ -60,11 +60,16 @@
     token_rows = req_dev * seq_len
     column = lax.axis_index("tensor")
     place = lax.axis_index("dp")
+
+    def clear_squares(chunk):
+        return jnp.concatenate(
+            jax.lax.all_to_all(jnp.stack([chunk] * jax.lax.axis_size("tensor"), 0), "tensor", 0, 0),
+            1,
+        )
+
     full_tokens, full_prefix = (
         lax.all_gather(tokens.reshape(token_rows, d_part), "tensor", axis=1, tiled=True),
-        lax.all_gather(
-            shared_prefix_tokens.reshape(grp_dev * pre_len, d_part), "tensor", axis=1, tiled=True
-        ),
+        clear_squares(shared_prefix_tokens.reshape(grp_dev * pre_len, d_part)),
     )
     normed_input = normalize(full_tokens, input_norm_gain)
     prefix_normed = normalize(full_prefix, input_norm_gain)

time: 345 us -> 366 us (1.061)
  waiting for transfers between devices: 188 us -> 202 us
  starting transfers between devices: 0.19 us -> 4.84 us
    all_to_all x0 -> x1, waiting for transfers between devices: none -> 49.7 us  [clear_squares(): jax.lax.all_to_all(jnp.stack([chunk] * jax.lax.axis_size('tensor'), 0), '...]
    all_gather x1 -> x0, waiting for transfers between devices: 35.6 us -> none  [on_device(): lax.all_gather(shared_prefix_tokens.reshape(grp_dev * pre_len, d_part), '...]
    all_to_all x0 -> x1, starting transfers between devices: none -> 4.69 us  [clear_squares(): jax.lax.all_to_all(jnp.stack([chunk] * jax.lax.axis_size('tensor'), 0), '...]
    convert_element_type x2 -> x3, other arithmetic: 8.99 us -> 11.3 us  [normalize(): return (values * scale * gain.astype(jnp.float32)).astype(jnp.bfloat16)]
    unnamed x37 -> x39, local copies, waits for them, and re-layouts: 14.3 us -> 14.2 us
  transfers between devices with their start and end apart: 5 -> 5, of which waited for: 5 -> 5; matrix products, arithmetic and copies ran while one was open for 12% -> 11% of each run, Pallas kernels for 0% -> 0%
where the time goes in v1:
time: 366 us
  waiting for transfers between devices  202 us (55%)
  matrix products  56.5 us (15%)
  other arithmetic  34.2 us (9%)
  local copies, waits for them, and re-layouts  28.5 us (8%)
  blocking collectives  25.3 us (7%)
  between operations  14.2 us (4%)
  starting transfers between devices  4.84 us (1%)
    all_gather x1, waiting for transfers between devices, on_device(): lax.all_gather(tokens.reshape(token_rows, d_part), 'tensor', axis=1, tile...  80.4 us
    all_to_all x1, waiting for transfers between devices, clear_squares(): jax.lax.all_to_all(jnp.stack([chunk] * jax.lax.axis_size('tensor'), 0), '...  49.7 us
    all_gather x1, waiting for transfers between devices, on_device(): lax.all_gather(jnp.stack([pre_keys, pre_vals], 1), 'dp', axis=0, tiled=True)  41.1 us
    all_gather x1, waiting for transfers between devices, on_device(): page_piece = lax.all_gather(adapter_down_weight, 'dp', axis=0, tiled=True)  29.1 us
    psum x1, blocking collectives, on_device(): low_rank_rows = lax.psum(partial_low, 'tensor').astype(jnp.bfloat16)  25.3 us
    dot_general x1, matrix products, on_device(): jnp.dot(normed_input, query_weight, preferred_element_type=jnp.float32)  22.6 us
    unnamed x39, local copies, waits for them, and re-layouts  14.2 us
    convert_element_type x3, other arithmetic, normalize(): return (values * scale * gain.astype(jnp.float32)).astype(jnp.bfloat16)  11.3 us
  transfers between devices with their start and end apart: 5, of which 5 were waited for; matrix products, arithmetic and copies ran while one was open for 11% of the time, Pallas kernels for 0%

profile of v1, /device:TPU:0, one launch (start us, length us, event | category | flops | bytes accessed | tf_op | source)
XLA Modules:
  0.0 365.9 jit_solution(2727654377425663415)
XLA Ops:
  7.2 1.4 copy.65
  8.6 2.3 stack.9
  10.8 4.7 %all-to-all-start = ((bf16[8,256,1024]{1,2,0:T(8,128)(2,1)}), bf16[8,256,1024]{1,2,0:T(8,128)(2,1)}, u32[]{:S(2)}, u32[]{:S(2)}) async-start(bf16[8,256,1024]{1,2,0:T(8,128)(2,1)} %stack.9), calls=%async_computation | async-start | bytes 8388608 | tf_op jit(solution)/shard_map/all_to_all | solution.py:66
  15.6 49.7 %all-to-all-done = bf16[8,256,1024]{1,2,0:T(8,128)(2,1)} async-done(((bf16[8,256,1024]{1,2,0:T(8,128)(2,1)}), bf16[8,256,1024]{1,2,0:T(8,128)(2,1)}, u32[]{:S(2)}, u32[]{:S(2)}) %all-to-all-start) | async-done | bytes 4194336 | tf_op jit(solution)/shard_map/all_to_all | solution.py:66
  65.3 3.3 multiply_reduce_fusion
  68.6 3.0 fusion.6
  71.6 1.0 convolution_bitcast_fusion
  72.7 1.0 fusion.28
  73.8 0.3 fusion.45
  74.1 0.8 copy.67
  75.0 0.7 all-gather.7.cloned.1.call-update
  75.7 0.7 all-gather.9.cloned.1.call-update
  76.4 0.5 all-gather.11.cloned.1.call-update
  77.0 0.2 select_reduce_fusion.1
  77.4 0.3 multiply_cosine_fusion
  77.7 0.6 iota_compare_fusion.3
  78.3 0.6 pad_clamp_fusion
  79.1 0.5 fusion.46
  79.6 41.1 %all-gather.5.cloned.1.call-done = bf16[16,2,256,128]{3,2,1,0:T(8,128)(2,1)} async-done(((bf16[1,2,256,128]{3,2,1,0:T(8,128)(2,1)}), bf16[16,2,256,128]{3,2,1,0:T(8,128)(2,1)}) %all-gather.5.cloned.1.call-update) | async-done | bytes 2097168 | tf_op jit(solution)/shard_map/all_gather | solution.py:90
  120.7 2.5 gather_fusion
  123.2 1.0 fusion.54
  124.2 2.0 copy.82
  126.2 80.4 %all-gather.7.cloned.1.call-done = bf16[1024,8192]{1,0:T(8,128)(2,1)} async-done(((bf16[1024,1024]{1,0:T(8,128)(2,1)}), bf16[1024,8192]{1,0:T(8,128)(2,1)}) %all-gather.7.cloned.1.call-update) | async-done | bytes 16777232 | tf_op jit(solution)/shard_map/all_gather | solution.py:71
  206.6 7.5 %fusion = f32[1024]{0:T(1024)S(1)} fusion(bf16[1024,8192]{1,0:T(8,128)(2,1)} %all-gather.7.cloned.1.call-done), kind=kLoop, calls=%fused_computation.4 | loop fusion | flops 25164800 | bytes 16781312 | tf_op jit(solution)/shard_map/reduce_sum | solution.py:34
  214.1 3.2 copy-done.2
  217.3 8.3 %fusion.2 = bf16[1024,8192]{1,0:T(8,128)(2,1)} fusion(bf16[1024,8192]{1,0:T(8,128)(2,1)S(1)} %copy-done.2, f32[8192]{0:T(1024)S(1)} %convert_element_type.127, f32[1024]{0:T(1024)S(1)} %add_rsqrt_fusion), kind=kLoop, calls=%fused_computation.6 | loop fusion | flops 33554432 | bytes 33591296 | tf_op jit(solution)/shard_map/convert_element_type | solution.py:35
  225.5 29.1 %all-gather.9.cloned.1.call-done = bf16[64,1024,16]{1,2,0:T(8,128)(2,1)} async-done(((bf16[4,1024,16]{1,2,0:T(8,128)(2,1)}), bf16[64,1024,16]{1,2,0:T(8,128)(2,1)}) %all-gather.9.cloned.1.call-update) | async-done | bytes 2097168 | tf_op jit(solution)/shard_map/all_gather | solution.py:98
  254.7 5.1 %select_reduce_fusion = f32[1024,16]{0,1:T(8,128)S(1)} fusion(pred[1024,64]{0,1:T(8,128)(4,1)S(1)} %get-tuple-element.23, bf16[64,1024,16]{1,2,0:T(8,128)(2,1)} %all-gather.9.cloned.1.call-done, bf16[1024,8192]{1,0:T(8,128)(2,1)} %fusion.2, s32[]{:T(128)S(6)} %select_n.72), kind=kOutput, calls=%fused_computation.26 | convolution fusion | flops 2149564416 | bytes 4325380 | tf_op jit(solution)/shard_map/td,ndr->tnr/dot_general | solution.py:100
  259.8 25.3 %psum.7 = bf16[1024,16]{0,1:T(8,128)(2,1)S(1)} all-reduce(f32[1024,16]{0,1:T(8,128)S(1)} %select_reduce_fusion), channel_id=1, replica_groups=mesh['dp'=16,'tensor'=8] {'tensor'}, use_global_device_ids=true, to_apply=%region_4.5 | all-reduce | flops 16384 | bytes 98304 | tf_op jit(solution)/shard_map/psum | solution.py:103
  285.1 8.5 %convolution_convert_fusion = bf16[1024,128]{1,0:T(8,128)(2,1)S(1)} fusion(bf16[1024,8192]{1,0:T(8,128)(2,1)} %fusion.2, bf16[8192,128]{1,0:T(8,128)(2,1)S(1)} %copy-done), kind=kOutput, calls=%fused_computation.37 | convolution fusion | flops 2147614720 | bytes 19136512 | tf_op jit(solution)/shard_map/dot_general | solution.py:128
  293.6 2.4 copy-done.3
  296.0 0.6 copy-done.12
  296.6 4.5 %fusion.55 = f32[1024,128]{1,0:T(8,128)S(1)} fusion(bf16[1024,8192]{1,0:T(8,128)(2,1)S(1)} %copy-done.3, bf16[8192,128]{1,0:T(8,128)(2,1)S(1)} %copy-done.12), kind=kOutput, calls=%fused_computation.98 | convolution fusion | flops 2147483648 | bytes 19398656 | tf_op jit(solution)/shard_map/dot_general | solution.py:123
  301.2 5.4 %fusion.11 = bf16[1024,1024]{1,0:T(8,128)(2,1)S(1)} fusion(bf16[64,16,1024]{2,1,0:T(8,128)(2,1)} %all-gather.11.cloned.1.call-done, bf16[1024,16]{0,1:T(8,128)(2,1)S(1)} %psum.7, bf16[1024,64]{0,1:T(8,128)(2,1)S(1)} %get-tuple-element.22), kind=kOutput, calls=%fused_computation.22 | convolution fusion | flops 2150629376 | bytes 4358144 | tf_op jit(solution)/shard_map/dot_general | solution.py:110
  306.7 22.6 %add_bitcast_fusion = f32[128,8,8,128]{3,1,2,0:T(8,128)S(1)} fusion(bf16[1024,1024]{1,0:T(8,128)(2,1)S(1)} %fusion.11, bf16[1024,8192]{1,0:T(8,128)(2,1)} %fusion.2, bf16[8192,1024]{1,0:T(8,128)(2,1)} %param.16), kind=kOutput, calls=%fused_computation.25 | convolution fusion | flops 17181966336 | bytes 39845888 | tf_op jit(solution)/shard_map/dot_general | solution.py:117
  329.2 1.0 copy.86
  330.2 4.6 %fusion.53 = (f32[8,128,8,64]{3,2,1,0:T(8,128)}, f32[8,128,8,64]{3,2,1,0:T(8,128)}) fusion(f32[8,128,8,128]{3,2,1,0:T(8,128)S(1)} %bitcast.98), kind=kLoop, calls=%fused_computation.96 | loop fusion | bytes 8388608 | tf_op jit(solution)/shard_map/slice | solution.py:23
  334.8 0.2 subtract_convert_fusion.1
  335.1 0.3 broadcast_select_fusion.1
  335.4 0.8 copy.69
  336.2 5.2 %subtract_convert_fusion = (bf16[8,128,8,64]{3,1,2,0:T(8,128)(2,1)S(1)}, bf16[8,128,8,64]{3,1,2,0:T(8,128)(2,1)S(1)}) fusion(f32[8,128,8,64]{3,2,1,0:T(8,128)} %get-tuple-element.15, f32[8,128,8,64]{3,2,1,0:T(8,128)} %get-tuple-element.14, f32[128,64]{1,0:T(8,128)S(1)} %get-tuple-element.29, f32[128,64]{1,0:T(8,128)S(1)} %get-tuple-element.28), kind=kLoop, calls=%fused_computation.24 | loop fusion | flops 4194304 | bytes 6356992 | tf_op jit(solution)/shard_map/convert.6
  341.5 3.1 fusion.4
  344.6 3.2 fusion.3
  347.8 5.3 %fusion.10 = bf16[8,1,128,8,128]{4,2,3,0,1:T(8,128)(2,1)} fusion(f32[8,8,128]{2,1,0:T(8,128)S(1)} %fusion.3, f32[8,8,128]{2,1,0:T(8,128)S(1)} %get-tuple-element.30, f32[8,384,128,8]{2,1,3,0:T(8,128)S(1)} %get-tuple-element.31, pred[128,384]{0,1:T(8,128)(4,1)S(1)} %fusion.35, pred[8,128]{1,0:T(8,128)(4,1)S(1)} %copy-done.9, ...), kind=kOutput, calls=%fused_computation.20 | convolution fusion | flops 824705024 | bytes 15582208 | tf_op jit(solution)/shard_map/bkgts,bskd->btkgd/dot_general | solution.py:152
  353.1 4.1 %copy.77 = bf16[8,128,1024]{2,1,0:T(8,128)(2,1)} copy(bf16[8,128,1024]{1,2,0:T(8,128)(2,1)} %bitcast.102) | data formatting | bytes 4194304
  357.2 0.3 maximum_select_fusion.1
  357.7 0.9 scatter_fusion
  358.6 0.8 copy-done.5
  (54 shorter events, 1.0 us)
Async XLA Ops:
  7.2 65.5 %copy-start = (bf16[8192,128]{1,0:T(8,128)(2,1)S(1)}, bf16[8192,128]{1,0:T(8,128)(2,1)}, u32[]{:S(2)}) copy-start(bf16[8192,128]{1,0:T(8,128)(2,1)} %param.18) | copy-start | bytes 6291460
  10.8 4.7 %copy-start.8 = (bf16[8192]{0:T(1024)(128)(2,1)S(1)}, bf16[8192]{0:T(1024)(128)(2,1)}, u32[]{:S(2)}) copy-start(bf16[8192]{0:T(1024)(128)(2,1)} %param.15) | copy-start | bytes 49156
  10.8 54.5 %all-to-all-start = ((bf16[8,256,1024]{1,2,0:T(8,128)(2,1)}), bf16[8,256,1024]{1,2,0:T(8,128)(2,1)}, u32[]{:S(2)}, u32[]{:S(2)}) async-start(bf16[8,256,1024]{1,2,0:T(8,128)(2,1)} %stack.9), calls=%async_computation | async-start | bytes 8388608 | tf_op jit(solution)/shard_map/all_to_all | solution.py:66
  15.5 105.2 %all-gather.5.cloned.1.call-start = ((), (), s32[]{:S(2)}) async-start(), calls=%async_computation.1 | async-start | bytes 2228224 | tf_op jit(solution)/shard_map/all_gather | solution.py:90
  68.6 3.0 copy-start.11
  72.7 4.3 %copy-start.13 = (s32[64]{0:T(128)S(1)}, s32[64]{0:T(128)}, u32[]{:S(2)}) copy-start(s32[64]{0:T(128)} %param.21) | copy-start | bytes 772
  72.7 4.3 %copy-start.14 = (s32[8]{0:T(128)S(1)}, s32[8]{0:T(128)}, u32[]{:S(2)}) copy-start(s32[8]{0:T(128)} %param.22) | copy-start | bytes 100
  72.7 5.0 %copy-start.15 = (s32[8]{0:T(128)S(1)}, s32[8]{0:T(128)}, u32[]{:S(2)}) copy-start(s32[8]{0:T(128)} %param.24) | copy-start | bytes 100
  72.7 5.6 %copy-start.16 = (s32[8]{0:T(128)S(1)}, s32[8]{0:T(128)}, u32[]{:S(2)}) copy-start(s32[8]{0:T(128)} %param.23) | copy-start | bytes 100
  72.7 6.4 %copy-start.17 = (s32[8,1]{0,1:T(1,128)S(1)}, s32[8,1]{0,1:T(1,128)}, u32[]{:S(2)}) copy-start(s32[8,1]{0,1:T(1,128)} %param.25) | copy-start | bytes 100
  74.9 131.7 %all-gather.7.cloned.1.call-start = ((), (), s32[]{:S(2)}) async-start(), calls=%async_computation.2 | async-start | bytes 18874368 | tf_op jit(solution)/shard_map/all_gather | solution.py:71
  75.7 179.0 %all-gather.9.cloned.1.call-start = ((), (), s32[]{:S(2)}) async-start(), calls=%async_computation.3 | async-start | bytes 2228224 | tf_op jit(solution)/shard_map/all_gather | solution.py:98
  76.4 224.8 %all-gather.11.cloned.1.call-start = ((), (), s32[]{:S(2)}) async-start(), calls=%async_computation.4 | async-start | bytes 2228224 | tf_op jit(solution)/shard_map/all_gather | solution.py:104
  206.6 10.7 %copy-start.2 = (bf16[1024,8192]{1,0:T(8,128)(2,1)S(1)}, bf16[1024,8192]{1,0:T(8,128)(2,1)}, u32[]{:S(2)}) copy-start(bf16[1024,8192]{1,0:T(8,128)(2,1)} %all-gather.7.cloned.1.call-done) | copy-start | bytes 50331652
  285.1 10.9 %copy-start.3 = (bf16[1024,8192]{1,0:T(8,128)(2,1)S(1)}, bf16[1024,8192]{1,0:T(8,128)(2,1)}, u32[]{:S(2)}) copy-start(bf16[1024,8192]{1,0:T(8,128)(2,1)} %fusion.2) | copy-start | bytes 50331652
  285.1 11.5 %copy-start.12 = (bf16[8192,128]{1,0:T(8,128)(2,1)S(1)}, bf16[8192,128]{1,0:T(8,128)(2,1)}, u32[]{:S(2)}) copy-start(bf16[8192,128]{1,0:T(8,128)(2,1)} %param.17) | copy-start | bytes 6291460
  330.2 4.8 %copy-start.9 = (pred[8,128]{1,0:T(8,128)(4,1)S(1)}, pred[8,128]{1,0:T(8,128)(4,1)}, u32[]{:S(2)}) copy-start(pred[8,128]{1,0:T(8,128)(4,1)} %iota_compare_fusion.3) | copy-start | bytes 3076
  336.2 5.2 %copy-start.4 = (bf16[8,256,1,128]{3,1,0,2:T(8,128)(2,1)S(1)}, bf16[8,256,1,128]{3,1,0,2:T(8,128)(2,1)}, u32[]{:S(2)}) copy-start(bf16[8,256,1,128]{3,1,0,2:T(8,128)(2,1)} %get-tuple-element.17) | copy-start | bytes 1572868
  344.6 3.2 copy-start.6
  344.6 3.2 copy-start.7
  353.1 4.6 %copy-start.10 = (s32[8]{0:T(128)S(1)}, s32[8]{0:T(128)}, u32[]{:S(2)}) copy-start(s32[8]{0:T(128)} %fusion.46) | copy-start | bytes 100
  353.1 6.2 %copy-start.1 = (bf16[8192,128]{1,0:T(8,128)(2,1)S(1)}, bf16[8192,128]{1,0:T(8,128)(2,1)}, u32[]{:S(2)}) copy-start(bf16[8192,128]{1,0:T(8,128)(2,1)} %param.18) | copy-start | bytes 6291460
  358.5 0.8 copy-start.5
Sparse Core Ops, SparseCore 0:
  75.0 45.6 all-gather.4
  122.4 84.1 all-gather.6
  208.8 45.8 all-gather.8
  256.7 44.5 all-gather.10
